TPU v7x, 256 devices: a whole 4x4x8 slice. The times are simulated.
256 devices in a mesh: scen: 64 (over y, z, core), link: 4 (over x).
Axes of the slice: x: 4, y: 4, z: 8, core: 2. Of those that a mesh axis runs over, the one named last changes fastest.
Arguments:
- factor_inv: bfloat16 [128, 1024, 1024], P('scen'), may hold values from -0.1875 to 0.1875
- coupling: bfloat16 [128, 1024, 1024], P('scen', None, 'link'), may hold values from -0.375 to 0.375
- first_diag: float32 [128, 128], P('scen'), may hold values from 1 to 10
- pattern: int32 [128, 8], P('scen'), may hold values from 0 to 127, as said below
Outputs:
- panel: float32 [16384, 128], P('scen')
- trailing: float32 [16384, 16384], P('scen', 'link')
Inputs may be any that keep to these rules, and one draw needn't show every extreme that they name: `pattern`: slot t of a scenario names a block of column range t // 2, that is, a block p with p // 32 = t // 2. The 2 scenarios of rows s * 2 to (s + 1) * 2 - 1 name every block at most once among them, and at most 1 block of any one group of blocks with the same p // 2. The first scenario of every such set names block 0 in slot 0.
All inputs are finite; a program needn't handle non-finite values.
Results may differ from a plain program's by a relative error of at most 0.0005.
Values may be sent and summed in bfloat16 or wider, within the bound.
No kernel may reach another device: no remote copies, remote signals or barrier semaphores. Data moves between devices by JAX's collectives and lax.ppermute only.
A program may use at most 128 MiB of HBM per device.

v0:
```python
import jax
import jax.numpy as jnp
from jax import lax
from jax.sharding import PartitionSpec as P


def broadcast(value, axis, source):
    kept = jnp.where(lax.axis_index(axis) == source, value, 0).astype(value.dtype)
    return lax.psum(kept, axis)


def per_device(factor_inv, coupling, first_diag, pattern):
    tile_size = first_diag.shape[1]
    rows_own = first_diag.shape[0]
    scen_count = lax.axis_size("scen")
    link_count = lax.axis_size("link")
    scen_pos = lax.axis_index("scen")
    link_pos = lax.axis_index("link")
    block_count = rows_own * scen_count
    per_link = block_count // link_count
    col_width = coupling.shape[2]
    slot_count = col_width // tile_size
    own_slabs = jnp.einsum(
        "snm,smc->snc", factor_inv, coupling, preferred_element_type=jnp.float32
    ).astype(jnp.bfloat16)
    contrib = jnp.einsum(
        "snr,snc->src",
        lax.all_gather(own_slabs, "link", axis=2, tiled=True),
        own_slabs,
        preferred_element_type=jnp.float32,
    )
    scen_here = contrib.shape[0]
    spread = pattern.shape[1]
    blocks = pattern.reshape(-1)
    tile_rows = contrib.reshape(scen_here * spread, tile_size, col_width)
    own_cols = (
        lax.dynamic_slice_in_dim(pattern, link_pos * slot_count, slot_count, 1)
        - link_pos * per_link
    )
    col_rows = jnp.broadcast_to(own_cols[:, None, :], (scen_here, spread, slot_count)).reshape(
        scen_here * spread, slot_count
    )
    col_range = jnp.arange(per_link, dtype=jnp.int32)
    outgoing = jnp.zeros((block_count, tile_size, col_width), jnp.float32).at[blocks].set(tile_rows)
    labels = jnp.full((block_count, slot_count), -1, jnp.int32).at[blocks].set(col_rows)
    arrived, arrived_cols = (
        lax.all_to_all(outgoing, "scen", split_axis=0, concat_axis=0, tiled=True),
        lax.all_to_all(labels, "scen", split_axis=0, concat_axis=0, tiled=True),
    )
    selector = (arrived_cols[:, :, None] == col_range[None, None, :]).astype(jnp.float32)
    selector = selector.reshape(scen_count, rows_own, slot_count, per_link)
    arrived = arrived.reshape(scen_count, rows_own, tile_size, slot_count, tile_size)
    summed = jnp.einsum("srkc,srxky->rxcy", selector, arrived, precision=lax.Precision.HIGHEST)
    global_rows = scen_pos * rows_own + jnp.arange(rows_own, dtype=jnp.int32)
    global_cols = link_pos * per_link + col_range
    on_diagonal = (global_rows[:, None] == global_cols[None, :]).astype(jnp.float32)
    unit_matrix = jnp.eye(tile_size, dtype=jnp.float32)
    diag_part = (
        on_diagonal[:, None, :, None]
        * (first_diag[:, :, None] * unit_matrix[None, :, :])[:, :, None, :]
    )
    schur = (summed + diag_part).reshape(rows_own * tile_size, per_link * tile_size)
    corner = broadcast(schur[:tile_size, :tile_size], "scen", 0)
    lead_factor = jnp.linalg.cholesky(corner)
    solved = jax.scipy.linalg.solve_triangular(lead_factor, schur[:, :tile_size].T, lower=True).T
    top_block = jnp.where(scen_pos == 0, lead_factor, solved[:tile_size])
    panel_mine = broadcast(jnp.concatenate([top_block, solved[tile_size:]], axis=0), "link", 0)
    gathered = lax.all_gather(panel_mine, "scen", axis=0, tiled=True)
    partner = lax.dynamic_slice_in_dim(
        gathered, link_pos * per_link * tile_size, per_link * tile_size, 0
    )
    trailing = schur - jnp.dot(
        panel_mine, partner.T, precision=lax.Precision.HIGHEST, preferred_element_type=jnp.float32
    )
    return (panel_mine, trailing)


def solution(mesh):
    in_specs = (P("scen", None, None), P("scen", None, "link"), P("scen", None), P("scen", None))
    out_specs = (P("scen", None), P("scen", "link"))
    return jax.shard_map(
        per_device, mesh=mesh, in_specs=in_specs, out_specs=out_specs, check_vma=False
    )
```

profile of v0, /device:TPU:1, one launch (start us, length us, event | category | flops | bytes accessed | tf_op | source)
XLA Modules:
  0.0 855.0 jit_solution(7507519871486025331)
XLA Ops:
  7.2 1.2 copy-done
  8.4 4.4 convolution_convert_fusion
  13.7 1.1 copy.30
  14.8 13.1 %all-to-all-start.1 = ((s32[64,2,2]{1,2,0:T(2,128)}), s32[64,2,2]{1,2,0:T(2,128)S(1)}, u32[]{:S(2)}, u32[]{:S(2)}) async-start(s32[64,2,2]{1,2,0:T(2,128)} %copy.30), calls=%async_computation.1 | async-start | bytes 131072 | tf_op jit(solution)/shard_map/all_to_all | solution.py:48
  27.9 41.4 %all-gather.3.cloned.1.call-done = bf16[2,1024,1024]{2,1,0:T(8,128)(2,1)} async-done(((bf16[2,1024,256]{2,1,0:T(8,128)(2,1)}), bf16[2,1024,1024]{2,1,0:T(8,128)(2,1)}) %all-gather.3.cloned.1.call-update) | async-done | bytes 4194320 | tf_op jit(solution)/shard_map/all_gather | solution.py:28
  69.3 4.2 fusion.15
  73.5 7.8 broadcast_in_dim.13
  81.4 3.7 scatter_fusion
  85.1 12.4 %all-to-all-start = ((f32[128,128,256]{2,1,0:T(8,128)}), f32[128,128,256]{2,1,0:T(8,128)}, u32[]{:S(2)}, u32[]{:S(2)}) async-start(f32[128,128,256]{2,1,0:T(8,128)} %scatter_fusion), calls=%async_computation | async-start | bytes 33554432 | tf_op jit(solution)/shard_map/all_to_all | solution.py:47
  98.0 365.0 %all-to-all-done = f32[128,128,256]{2,1,0:T(8,128)} async-done(((f32[128,128,256]{2,1,0:T(8,128)}), f32[128,128,256]{2,1,0:T(8,128)}, u32[]{:S(2)}, u32[]{:S(2)}) %all-to-all-start) | async-done | bytes 16777248 | tf_op jit(solution)/shard_map/all_to_all | solution.py:47
  463.0 17.4 %copy.26 = f32[128,128,256]{1,2,0:T(8,128)} copy(f32[128,128,256]{2,1,0:T(8,128)} %all-to-all-done) | data formatting | bytes 33554432 | tf_op jit(solution)/shard_map/all_to_all | solution.py:47
  480.4 16.5 %copy.32 = f32[64,2,128,2,128]{4,0,3,2,1:T(8,128)} copy(f32[64,2,128,2,128]{2,4,3,1,0:T(8,128)} %bitcast.40) | data formatting | bytes 33554432 | tf_op jit(solution)/shard_map/reshape | solution.py:52
  496.9 9.5 %bitcast_add_fusion = f32[2,128,32,128]{3,2,1,0:T(8,128)S(1)} fusion(f32[64,2,128,2,128]{4,0,3,2,1:T(8,128)} %copy.32, f32[2,128,128]{2,1,0:T(8,128)S(1)} %broadcast_multiply_fusion, f32[2,32]{1,0:T(2,128)S(1)} %compare_convert_fusion, s32[64,2,2]{0,2,1:T(2,128)S(1)} %copy.31), kind=kOutput, calls=%fused_computation.4 | convolution fusion | flops 1612718080 | bytes 21103872 | tf_op jit(solution)/shard_map/srkc,srxky->rxcy/dot_general | solution.py:53
  506.5 3.9 copy.45
  510.4 2.0 copy-done.3
  513.3 167.0 %all-reduce.3.cloned.1.call-done = f32[128,128]{1,0:T(8,128)} async-done(((f32[128,128]{1,0:T(8,128)}), f32[128,128]{1,0:T(8,128)}) %all-reduce.3.cloned.1.call-update) | async-done | bytes 65552 | tf_op jit(solution)/shard_map/psum | solution.py:9
  680.3 0.9 copy.33
  681.2 0.9 fusion.4
  682.1 11.7 %cholesky.19 = f32[128,128]{1,0:T(8,128)S(1)} custom-call(f32[128,128]{1,0:T(8,128)S(1)} %fusion.4), custom_call_target="Cholesky" | custom-call | tf_op jit(solution)/shard_map/jit(cholesky)/cholesky | solution.py:64
  695.1 9.8 %custom-call.7 = f32[1,128,128]{1,2,0:T(8,128)S(1)} custom-call(f32[1,128,128]{2,1,0:T(8,128)S(1)} %select_bitcast_fusion), custom_call_target="InvertDiagBlocksLowerTriangular" | custom-call | tf_op jit(solution)/shard_map/jit(_solve_triangular)/triangular_solve | solution.py:65
  704.9 1.2 fusion.1
  707.8 41.0 %all-reduce.5.cloned.1.call-done = f32[256,128]{1,0:T(8,128)} async-done(((f32[256,128]{1,0:T(8,128)}), f32[256,128]{1,0:T(8,128)}) %all-reduce.5.cloned.1.call-update) | async-done | bytes 131088 | tf_op jit(solution)/shard_map/psum | solution.py:9
  748.8 88.6 %all-gather.5.cloned.1.call-done = f32[16384,128]{1,0:T(8,128)} async-done(((f32[256,128]{1,0:T(8,128)}), f32[16384,128]{1,0:T(8,128)}) %all-gather.5.cloned.1.call-update) | async-done | bytes 8388624 | tf_op jit(solution)/shard_map/all_gather | solution.py:68
  837.4 10.4 %convolution_subtract_fusion = f32[256,4096]{1,0:T(8,128)} fusion(f32[256,128]{1,0:T(8,128)} %all-reduce.5.cloned.1.call-done, f32[16384,128]{1,0:T(8,128)} %all-gather.5.cloned.1.call-done, s32[]{:T(128)S(6)} %select_n.51, f32[32,8,32,128]{3,2,1,0:T(8,128)} %bitcast.42), kind=kOutput, calls=%fused_computation.2 | convolution fusion | flops 1611661312 | bytes 10616836 | tf_op jit(solution)/shard_map/dot_general | solution.py:72
  (38 shorter events, 6.0 us)
Async XLA Ops:
  7.2 1.2 copy-start
  7.2 5.7 copy-start.6
  7.2 62.1 %all-gather.3.cloned.1.call-start = ((), (), s32[]{:S(2)}) async-start(), calls=%async_computation.2 | async-start | bytes 5242880 | tf_op jit(solution)/shard_map/all_gather | solution.py:28
  14.8 70.3 %all-to-all-start.1 = ((s32[64,2,2]{1,2,0:T(2,128)}), s32[64,2,2]{1,2,0:T(2,128)S(1)}, u32[]{:S(2)}, u32[]{:S(2)}) async-start(s32[64,2,2]{1,2,0:T(2,128)} %copy.30), calls=%async_computation.1 | async-start | bytes 131072 | tf_op jit(solution)/shard_map/all_to_all | solution.py:48
  85.1 12.8 %copy-start.5 = (f32[2,128]{1,0:T(2,128)S(1)}, f32[2,128]{1,0:T(2,128)}, u32[]{:S(2)}) copy-start(f32[2,128]{1,0:T(2,128)} %param.6) | copy-start | bytes 3076
  85.1 377.9 %all-to-all-start = ((f32[128,128,256]{2,1,0:T(8,128)}), f32[128,128,256]{2,1,0:T(8,128)}, u32[]{:S(2)}, u32[]{:S(2)}) async-start(f32[128,128,256]{2,1,0:T(8,128)} %scatter_fusion), calls=%async_computation | async-start | bytes 33554432 | tf_op jit(solution)/shard_map/all_to_all | solution.py:47
  97.5 582.8 %all-reduce.3.cloned.1.call-start = ((), (), s32[]{:S(2)}) async-start(), calls=%async_computation.3 | async-start | bytes 131072 | tf_op jit(solution)/shard_map/psum | solution.py:9
  506.4 3.9 copy-start.2
  510.4 2.0 copy-start.3
  513.0 235.7 %all-reduce.5.cloned.1.call-start = ((), (), s32[]{:S(2)}) async-start(), calls=%async_computation.4 | async-start | bytes 262144 | tf_op jit(solution)/shard_map/psum | solution.py:9
  707.5 129.9 %all-gather.5.cloned.1.call-start = ((), (), s32[]{:S(2)}) async-start(), calls=%async_computation.5 | async-start | bytes 8519680 | tf_op jit(solution)/shard_map/all_gather | solution.py:68
  748.8 99.7 %copy-start.1 = (bf16[2,1024,256]{2,1,0:T(8,128)(2,1)S(1)}, bf16[2,1024,256]{2,1,0:T(8,128)(2,1)}, u32[]{:S(2)}) copy-start(bf16[2,1024,256]{2,1,0:T(8,128)(2,1)} %param.5) | copy-start | bytes 3145732
  748.8 99.0 %copy-start.4 = (f32[256,128]{1,0:T(8,128)S(1)}, f32[256,128]{1,0:T(8,128)}, u32[]{:S(2)}) copy-start(f32[256,128]{1,0:T(8,128)} %all-reduce.5.cloned.1.call-done) | copy-start | bytes 393220
Sparse Core Ops, SparseCore 0:
  12.9 56.2 all-gather.2
  513.2 167.0 all-reduce.2
  707.6 41.0 all-reduce.4
  751.4 85.9 all-gather.4
where the time goes:
time: 856 us; the launch traced here: 855 us
  waiting for transfers between devices  703 us (82%)
  local copies, waits for them, and re-layouts  56.1 us (7%)
  matrix products  29.7 us (3%)
  starting transfers between devices  26.4 us (3%)
  other arithmetic  25.9 us (3%)
  between operations  14 us (2%)
    all_to_all x1, waiting for transfers between devices, per_device(): lax.all_to_all(outgoing, 'scen', split_axis=0, concat_axis=0, tiled=True)  365 us
    psum x2, waiting for transfers between devices, broadcast(): return lax.psum(kept, axis)  208 us
    all_gather x1, waiting for transfers between devices, per_device(): gathered = lax.all_gather(panel_mine, 'scen', axis=0, tiled=True)  88.6 us
    all_gather x1, waiting for transfers between devices, per_device(): lax.all_gather(own_slabs, 'link', axis=2, tiled=True)  41.4 us
    all_to_all x1, local copies, waits for them, and re-layouts, per_device(): lax.all_to_all(outgoing, 'scen', split_axis=0, concat_axis=0, tiled=True)  17.4 us
  transfers between devices with their start and end apart: 6, of which 5 were waited for; matrix products, arithmetic and copies ran while one was open for 2% of the time, Pallas kernels for 0%

commit v1 on v0

--- a/solution.py
+++ b/solution.py
@@ -65,7 +65,9 @@
     solved = jax.scipy.linalg.solve_triangular(lead_factor, schur[:, :tile_size].T, lower=True).T
     top_block = jnp.where(scen_pos == 0, lead_factor, solved[:tile_size])
     panel_mine = broadcast(jnp.concatenate([top_block, solved[tile_size:]], axis=0), "link", 0)
-    gathered = lax.all_gather(panel_mine, "scen", axis=0, tiled=True)
+    gathered = jnp.concatenate(
+        lax.all_to_all(jnp.stack([panel_mine] * lax.axis_size("scen")), "scen", 0, 0), axis=0
+    )
     partner = lax.dynamic_slice_in_dim(
         gathered, link_pos * per_link * tile_size, per_link * tile_size, 0
     )

time: 856 us -> 971 us (1.13)
  waiting for transfers between devices: 703 us -> 800 us
  starting transfers between devices: 26.4 us -> 39.1 us
    all_to_all x0 -> x1, waiting for transfers between devices: none -> 186 us  [per_device(): lax.all_to_all(jnp.stack([panel_mine] * lax.axis_size('scen')), 'scen', 0...]
    all_gather x1 -> x0, waiting for transfers between devices: 88.6 us -> none  [per_device(): gathered = lax.all_gather(panel_mine, 'scen', axis=0, tiled=True)]
    all_to_all x0 -> x1, starting transfers between devices: none -> 13.1 us  [per_device(): lax.all_to_all(jnp.stack([panel_mine] * lax.axis_size('scen')), 'scen', 0...]
where the time goes in v1:
time: 971 us; the launch traced here: 970 us
  waiting for transfers between devices  800 us (82%)
  local copies, waits for them, and re-layouts  61.1 us (6%)
  starting transfers between devices  39.1 us (4%)
  matrix products  29.4 us (3%)
  other arithmetic  25.9 us (3%)
  between operations  13.9 us (1%)
    all_to_all x1, waiting for transfers between devices, per_device(): lax.all_to_all(outgoing, 'scen', split_axis=0, concat_axis=0, tiled=True)  365 us
    psum x2, waiting for transfers between devices, broadcast(): return lax.psum(kept, axis)  208 us
    all_to_all x1, waiting for transfers between devices, per_device(): lax.all_to_all(jnp.stack([panel_mine] * lax.axis_size('scen')), 'scen', 0...  186 us
    all_gather x1, waiting for transfers between devices, per_device(): lax.all_gather(own_slabs, 'link', axis=2, tiled=True)  41.4 us
  transfers between devices with their start and end apart: 6, of which 5 were waited for; matrix products, arithmetic and copies ran while one was open for 2% of the time, Pallas kernels for 0%

profile of v1, /device:TPU:1, one launch (start us, length us, event | category | flops | bytes accessed | tf_op | source)
XLA Modules:
  0.0 969.9 jit_solution(7598043602648062553)
XLA Ops:
  7.2 1.2 copy-done
  8.4 4.4 convolution_convert_fusion
  13.7 1.1 copy.30
  14.8 13.1 %all-to-all-start.1 = ((s32[64,2,2]{1,2,0:T(2,128)}), s32[64,2,2]{1,2,0:T(2,128)S(1)}, u32[]{:S(2)}, u32[]{:S(2)}) async-start(s32[64,2,2]{1,2,0:T(2,128)} %copy.30), calls=%async_computation.1 | async-start | bytes 131072 | tf_op jit(solution)/shard_map/all_to_all | solution.py:48
  27.9 41.4 %all-gather.2.cloned.1.call-done = bf16[2,1024,1024]{2,1,0:T(8,128)(2,1)} async-done(((bf16[2,1024,256]{2,1,0:T(8,128)(2,1)}), bf16[2,1024,1024]{2,1,0:T(8,128)(2,1)}) %all-gather.2.cloned.1.call-update) | async-done | bytes 4194320 | tf_op jit(solution)/shard_map/all_gather | solution.py:28
  69.3 4.2 fusion.15
  73.5 7.8 broadcast_in_dim.13
  81.4 3.7 scatter_fusion
  85.1 12.4 %all-to-all-start = ((f32[128,128,256]{2,1,0:T(8,128)}), f32[128,128,256]{2,1,0:T(8,128)}, u32[]{:S(2)}, u32[]{:S(2)}) async-start(f32[128,128,256]{2,1,0:T(8,128)} %scatter_fusion), calls=%async_computation | async-start | bytes 33554432 | tf_op jit(solution)/shard_map/all_to_all | solution.py:47
  98.0 365.0 %all-to-all-done = f32[128,128,256]{2,1,0:T(8,128)} async-done(((f32[128,128,256]{2,1,0:T(8,128)}), f32[128,128,256]{2,1,0:T(8,128)}, u32[]{:S(2)}, u32[]{:S(2)}) %all-to-all-start) | async-done | bytes 16777248 | tf_op jit(solution)/shard_map/all_to_all | solution.py:47
  463.0 17.4 %copy.26 = f32[128,128,256]{1,2,0:T(8,128)} copy(f32[128,128,256]{2,1,0:T(8,128)} %all-to-all-done) | data formatting | bytes 33554432 | tf_op jit(solution)/shard_map/all_to_all | solution.py:47
  480.3 16.5 %copy.32 = f32[64,2,128,2,128]{4,0,3,2,1:T(8,128)} copy(f32[64,2,128,2,128]{2,4,3,1,0:T(8,128)} %bitcast.41) | data formatting | bytes 33554432 | tf_op jit(solution)/shard_map/reshape | solution.py:52
  496.8 9.5 bitcast_add_fusion
  506.4 3.9 copy.45
  510.3 2.0 copy-done.3
  513.2 167.0 %all-reduce.3.cloned.1.call-done = f32[128,128]{1,0:T(8,128)} async-done(((f32[128,128]{1,0:T(8,128)}), f32[128,128]{1,0:T(8,128)}) %all-reduce.3.cloned.1.call-update) | async-done | bytes 65552 | tf_op jit(solution)/shard_map/psum | solution.py:9
  682.0 11.7 %cholesky.19 = f32[128,128]{1,0:T(8,128)S(1)} custom-call(f32[128,128]{1,0:T(8,128)S(1)} %fusion.4), custom_call_target="Cholesky" | custom-call | tf_op jit(solution)/shard_map/jit(cholesky)/cholesky | solution.py:64
  695.0 9.8 %custom-call.7 = f32[1,128,128]{1,2,0:T(8,128)S(1)} custom-call(f32[1,128,128]{2,1,0:T(8,128)S(1)} %select_bitcast_fusion), custom_call_target="InvertDiagBlocksLowerTriangular" | custom-call | tf_op jit(solution)/shard_map/jit(_solve_triangular)/triangular_solve | solution.py:65
  704.8 1.2 fusion.1
  707.4 41.3 %all-reduce.5.cloned.1.call-done = f32[256,128]{1,0:T(8,128)} async-done(((f32[256,128]{1,0:T(8,128)}), f32[256,128]{1,0:T(8,128)}) %all-reduce.5.cloned.1.call-update) | async-done | bytes 131088 | tf_op jit(solution)/shard_map/psum | solution.py:9
  748.6 5.1 stack.2
  753.8 13.1 %all-to-all-start.2 = ((f32[64,256,128]{2,1,0:T(8,128)}), f32[64,256,128]{2,1,0:T(8,128)}, u32[]{:S(2)}, u32[]{:S(2)}) async-start(f32[64,256,128]{2,1,0:T(8,128)} %stack.2), calls=%async_computation.2 | async-start | bytes 16777216 | tf_op jit(solution)/shard_map/all_to_all | solution.py:69
  766.8 185.7 %all-to-all-done.2 = f32[64,256,128]{2,1,0:T(8,128)} async-done(((f32[64,256,128]{2,1,0:T(8,128)}), f32[64,256,128]{2,1,0:T(8,128)}, u32[]{:S(2)}, u32[]{:S(2)}) %all-to-all-start.2) | async-done | bytes 8388640 | tf_op jit(solution)/shard_map/all_to_all | solution.py:69
  952.6 10.1 %convolution_subtract_fusion = f32[256,4096]{1,0:T(8,128)} fusion(f32[256,128]{1,0:T(8,128)S(1)} %copy-done.4, f32[16384,128]{1,0:T(8,128)} %bitcast.13, s32[]{:T(128)S(6)} %select_n.51, f32[32,8,32,128]{3,2,1,0:T(8,128)} %bitcast.43), kind=kOutput, calls=%fused_computation.2 | convolution fusion | flops 1611661312 | bytes 10616836 | tf_op jit(solution)/shard_map/dot_general | solution.py:74
  (38 shorter events, 7.4 us)
Async XLA Ops:
  7.2 1.2 copy-start
  7.2 5.7 copy-start.6
  7.2 62.1 %all-gather.2.cloned.1.call-start = ((), (), s32[]{:S(2)}) async-start(), calls=%async_computation.3 | async-start | bytes 5242880 | tf_op jit(solution)/shard_map/all_gather | solution.py:28
  14.8 70.3 %all-to-all-start.1 = ((s32[64,2,2]{1,2,0:T(2,128)}), s32[64,2,2]{1,2,0:T(2,128)S(1)}, u32[]{:S(2)}, u32[]{:S(2)}) async-start(s32[64,2,2]{1,2,0:T(2,128)} %copy.30), calls=%async_computation.1 | async-start | bytes 131072 | tf_op jit(solution)/shard_map/all_to_all | solution.py:48
  85.1 12.8 %copy-start.5 = (f32[2,128]{1,0:T(2,128)S(1)}, f32[2,128]{1,0:T(2,128)}, u32[]{:S(2)}) copy-start(f32[2,128]{1,0:T(2,128)} %param.6) | copy-start | bytes 3076
  85.1 377.9 %all-to-all-start = ((f32[128,128,256]{2,1,0:T(8,128)}), f32[128,128,256]{2,1,0:T(8,128)}, u32[]{:S(2)}, u32[]{:S(2)}) async-start(f32[128,128,256]{2,1,0:T(8,128)} %scatter_fusion), calls=%async_computation | async-start | bytes 33554432 | tf_op jit(solution)/shard_map/all_to_all | solution.py:47
  97.5 582.7 %all-reduce.3.cloned.1.call-start = ((), (), s32[]{:S(2)}) async-start(), calls=%async_computation.4 | async-start | bytes 131072 | tf_op jit(solution)/shard_map/psum | solution.py:9
  506.3 3.9 copy-start.2
  510.2 2.0 copy-start.3
  512.9 235.7 %all-reduce.5.cloned.1.call-start = ((), (), s32[]{:S(2)}) async-start(), calls=%async_computation.5 | async-start | bytes 262144 | tf_op jit(solution)/shard_map/psum | solution.py:9
  753.8 198.8 %copy-start.4 = (f32[256,128]{1,0:T(8,128)S(1)}, f32[256,128]{1,0:T(8,128)}, u32[]{:S(2)}) copy-start(f32[256,128]{1,0:T(8,128)} %all-reduce.5.cloned.1.call-done) | copy-start | bytes 393220
  753.8 198.8 %all-to-all-start.2 = ((f32[64,256,128]{2,1,0:T(8,128)}), f32[64,256,128]{2,1,0:T(8,128)}, u32[]{:S(2)}, u32[]{:S(2)}) async-start(f32[64,256,128]{2,1,0:T(8,128)} %stack.2), calls=%async_computation.2 | async-start | bytes 16777216 | tf_op jit(solution)/shard_map/all_to_all | solution.py:69
  952.6 10.8 %copy-start.1 = (bf16[2,1024,256]{2,1,0:T(8,128)(2,1)S(1)}, bf16[2,1024,256]{2,1,0:T(8,128)(2,1)}, u32[]{:S(2)}) copy-start(bf16[2,1024,256]{2,1,0:T(8,128)(2,1)} %param.5) | copy-start | bytes 3145732
Sparse Core Ops, SparseCore 0:
  12.9 56.2 all-gather.1
  513.0 167.0 all-reduce.2
  707.5 41.0 all-reduce.4
